TPU v7x, 32 devices: a whole 2x2x4 slice. The times are simulated.
32 devices in a mesh: dp: 8 (over z, x), mp: 4 (over y, core).
Axes of the slice: x: 2, y: 2, z: 4, core: 2. Of those that a mesh axis runs over, the one named last changes fastest.
Arguments:
- rows: float32 [16384, 1280], P(('dp', 'mp')), may hold values from -6 to 6
- lengths: int32 [256], P('dp'), may hold values from 1 to 64, as said below
- freq_class: int32 [256], P(('dp', 'mp')), may hold values from 0 to 2
- freq_table: float32 [3, 1280], replicated, may hold values from -3 to 3
- gain_attn: float32 [1280], replicated, may hold values from 0.5 to 1.5
- gain_mlp: float32 [1280], replicated, may hold values from 0.5 to 1.5
- w_qkv: float32 [3, 1280, 1280], P(None, None, 'mp'), may hold values from -0.15625 to 0.15625
- w_out: float32 [1280, 1280], P('mp'), may hold values from -0.5 to 0.5
- w_gate_up: float32 [2, 1280, 5120], P(None, None, 'mp'), may hold values from -0.15625 to 0.15625
- w_down: float32 [5120, 1280], P('mp'), may hold values from -0.15625 to 0.15625
- cotangent: float32 [16384, 1280], P(('dp', 'mp')), may hold values from -6 to 6
Outputs:
- output: float32 [16384, 1280], P(('dp', 'mp'))
- grad_rows: float32 [16384, 1280], P(('dp', 'mp'))
- grad_qkv: float32 [3, 1280, 1280], P(None, None, 'mp')
- grad_out: float32 [1280, 1280], P('mp')
- grad_gate_up: float32 [2, 1280, 5120], P(None, None, 'mp')
- grad_down: float32 [5120, 1280], P('mp')
- grad_gain_attn: float32 [1280], replicated
- grad_gain_mlp: float32 [1280], replicated
- grad_table: float32 [3, 1280], replicated
Inputs may be any that keep to these rules, and one draw needn't show every extreme that they name: `lengths`: the valid patches of a series are the last of its 64 slots; some series has all 64, and some only one.
All inputs are finite; a program needn't handle non-finite values.
Results may differ from a plain program's by a relative error of at most 0.02.
Values may be sent and summed in bfloat16 or wider, within the bound.
A program may use at most 256 MiB of HBM per device.

v0:
```python
import jax
import jax.numpy as jnp
from jax import lax
from jax.sharding import PartitionSpec as P

HS = 80
NFREQ = 3
SEQ = 64
EPSILON = 1e-06
NEGATIVE = -1e30
HIGHEST = lax.Precision.HIGHEST


def rotate(values, cosines, sines):
    half_width = values.shape[-1] // 2
    first_half = values[..., :half_width]
    second_half = values[..., half_width:]
    return jnp.concatenate(
        [first_half * cosines - second_half * sines, second_half * cosines + first_half * sines], -1
    )


def series_tables(series_lengths):
    places = jnp.arange(SEQ, dtype=jnp.int32)
    starts = SEQ - series_lengths
    valid_mask = places[None, :] >= starts[:, None]
    positions = (places[None, :] - starts[:, None]).astype(jnp.float32)
    frequency = 10000.0 ** (-2.0 * jnp.arange(HS // 2, dtype=jnp.float32) / HS)
    angles = positions[:, :, None] * frequency[None, None, :]
    return (valid_mask, jnp.cos(angles)[:, :, None, :], jnp.sin(angles)[:, :, None, :])


def allowed_pairs(valid_mask):
    places = jnp.arange(SEQ, dtype=jnp.int32)
    causal = places[:, None] >= places[None, :]
    itself = places[:, None] == places[None, :]
    return causal[None, None] & (valid_mask[:, None, None, :] | itself[None, None])


def norm_forward(values, gain):
    inverse = lax.rsqrt(jnp.mean(values * values, -1, keepdims=True) + EPSILON)
    return ((values * inverse * gain).astype(jnp.bfloat16), inverse)


def norm_backward(values, inverse, gain, grad_normed):
    normal = values * inverse
    grad_gain = jnp.sum(grad_normed * normal, 0)
    scaled = grad_normed * gain
    grad_values = inverse * (scaled - normal * jnp.mean(scaled * normal, -1, keepdims=True))
    return (grad_values, grad_gain)


def attention_scores(queries, keys, allowed):
    raw_scores = jnp.einsum("sihe,sjhe->shij", queries, keys, preferred_element_type=jnp.float32)
    return jnp.where(allowed, raw_scores * HS ** (-0.5), NEGATIVE)


def body(
    rows,
    lengths,
    freq_class,
    freq_table,
    gain_attn,
    gain_mlp,
    w_qkv,
    w_out,
    w_gate_up,
    w_down,
    cotangent,
):
    local_rows = rows.shape[0]
    mp_index = lax.axis_index("mp")
    series_count = lengths.shape[0]
    group_rows = series_count * SEQ
    heads_width = w_out.shape[0]
    head_count = heads_width // HS
    valid_mask, cosines, sines = series_tables(lengths)
    allowed = allowed_pairs(valid_mask)
    flat_valid = valid_mask.reshape(group_rows).astype(jnp.float32)
    mine_valid = lax.dynamic_slice_in_dim(flat_valid, mp_index * local_rows, local_rows)[:, None]
    classes = jnp.repeat(freq_class, SEQ)
    onehot = (classes[:, None] == jnp.arange(NFREQ, dtype=jnp.int32)[None, :]).astype(jnp.float32)
    start_rows = rows + jnp.dot(onehot, freq_table, precision=HIGHEST)
    normed_mine, inverse_attn = norm_forward(start_rows, gain_attn)
    normed = lax.all_gather(normed_mine, "mp", axis=0, tiled=True)
    qkv_low = w_qkv.astype(jnp.bfloat16)
    projected = jnp.einsum("td,cdf->ctf", normed, qkv_low, preferred_element_type=jnp.float32)
    projected = projected.reshape(3, series_count, SEQ, head_count, HS)
    queries = rotate(projected[0], cosines, sines).astype(jnp.bfloat16)
    keys = rotate(projected[1], cosines, sines).astype(jnp.bfloat16)
    values = projected[2].astype(jnp.bfloat16)
    scores = attention_scores(queries, keys, allowed)
    row_max = jnp.max(scores, -1, keepdims=True)
    exponent = jnp.exp(scores - row_max)
    row_total = jnp.sum(exponent, -1, keepdims=True)
    log_total = row_max + jnp.log(row_total)
    attention = (exponent / row_total).astype(jnp.bfloat16)
    mixed = jnp.einsum("shij,sjhe->sihe", attention, values, preferred_element_type=jnp.float32)
    mixed = mixed.reshape(group_rows, heads_width).astype(jnp.bfloat16)
    out_low = w_out.astype(jnp.bfloat16)
    attn_part = jnp.dot(mixed, out_low, preferred_element_type=jnp.float32)
    after_attn = start_rows + lax.psum_scatter(
        attn_part.astype(jnp.bfloat16), "mp", scatter_dimension=0, tiled=True
    ).astype(jnp.float32)
    normed_mlp_mine, inverse_mlp = norm_forward(after_attn, gain_mlp)
    normed_mlp = lax.all_gather(normed_mlp_mine, "mp", axis=0, tiled=True)
    gate_up_low = w_gate_up.astype(jnp.bfloat16)
    gate_up = jnp.einsum("td,cdf->ctf", normed_mlp, gate_up_low, preferred_element_type=jnp.float32)
    gate_pre = gate_up[0]
    up_pre = gate_up[1]
    sigmoid_gate = jax.nn.sigmoid(gate_pre)
    activated = gate_pre * sigmoid_gate
    hidden = (activated * up_pre).astype(jnp.bfloat16)
    down_low = w_down.astype(jnp.bfloat16)
    mlp_part = jnp.dot(hidden, down_low, preferred_element_type=jnp.float32)
    output = after_attn + lax.psum_scatter(
        mlp_part.astype(jnp.bfloat16), "mp", scatter_dimension=0, tiled=True
    ).astype(jnp.float32)
    grad_output = cotangent * mine_valid
    grad_down_in = lax.all_gather(grad_output.astype(jnp.bfloat16), "mp", axis=0, tiled=True)
    grad_down = jnp.einsum("tf,td->fd", hidden, grad_down_in, preferred_element_type=jnp.float32)
    grad_hidden = jnp.einsum(
        "td,fd->tf", grad_down_in, down_low, preferred_element_type=jnp.float32
    )
    grad_gate = grad_hidden * up_pre * (sigmoid_gate * (1.0 + gate_pre * (1.0 - sigmoid_gate)))
    grad_up = grad_hidden * activated
    grad_pre = jnp.stack([grad_gate, grad_up]).astype(jnp.bfloat16)
    grad_gate_up = jnp.einsum(
        "td,ctf->cdf", normed_mlp, grad_pre, preferred_element_type=jnp.float32
    )
    mlp_back_part = jnp.einsum(
        "ctf,cdf->td", grad_pre, gate_up_low, preferred_element_type=jnp.float32
    )
    grad_normed_mlp = lax.psum_scatter(
        mlp_back_part.astype(jnp.bfloat16), "mp", scatter_dimension=0, tiled=True
    ).astype(jnp.float32)
    grad_rows_mlp, grad_gain_mlp = norm_backward(after_attn, inverse_mlp, gain_mlp, grad_normed_mlp)
    grad_after = grad_output + grad_rows_mlp
    grad_attn_in = lax.all_gather(grad_after.astype(jnp.bfloat16), "mp", axis=0, tiled=True)
    grad_out = jnp.einsum("tf,td->fd", mixed, grad_attn_in, preferred_element_type=jnp.float32)
    grad_mixed = jnp.einsum("td,fd->tf", grad_attn_in, out_low, preferred_element_type=jnp.float32)
    grad_mixed = grad_mixed.astype(jnp.bfloat16).reshape(series_count, SEQ, head_count, HS)
    attention_again = jnp.exp(attention_scores(queries, keys, allowed) - log_total)
    grad_attention = jnp.einsum(
        "sihe,sjhe->shij", grad_mixed, values, preferred_element_type=jnp.float32
    )
    grad_values = jnp.einsum(
        "shij,sihe->sjhe",
        attention_again.astype(jnp.bfloat16),
        grad_mixed,
        preferred_element_type=jnp.float32,
    )
    row_dot = jnp.sum(attention_again * grad_attention, -1, keepdims=True)
    grad_scores = (attention_again * (grad_attention - row_dot)).astype(jnp.bfloat16)
    grad_queries = jnp.einsum(
        "shij,sjhe->sihe", grad_scores, keys, preferred_element_type=jnp.float32
    ) * HS ** (-0.5)
    grad_keys = jnp.einsum(
        "shij,sihe->sjhe", grad_scores, queries, preferred_element_type=jnp.float32
    ) * HS ** (-0.5)
    grad_projected = jnp.stack(
        [rotate(grad_queries, cosines, -sines), rotate(grad_keys, cosines, -sines), grad_values]
    )
    grad_projected = grad_projected.reshape(3, group_rows, heads_width).astype(jnp.bfloat16)
    grad_qkv = jnp.einsum("td,ctf->cdf", normed, grad_projected, preferred_element_type=jnp.float32)
    attn_back_part = jnp.einsum(
        "ctf,cdf->td", grad_projected, qkv_low, preferred_element_type=jnp.float32
    )
    grad_normed = lax.psum_scatter(
        attn_back_part.astype(jnp.bfloat16), "mp", scatter_dimension=0, tiled=True
    ).astype(jnp.float32)
    grad_rows_attn, grad_gain_attn = norm_backward(start_rows, inverse_attn, gain_attn, grad_normed)
    grad_rows = grad_after + grad_rows_attn
    grad_table = jnp.dot(onehot.T, grad_rows, precision=HIGHEST)
    grad_gain_attn, grad_gain_mlp, grad_table, token_total = lax.psum(
        (grad_gain_attn, grad_gain_mlp, grad_table, jnp.sum(mine_valid)), ("dp", "mp")
    )
    grad_qkv, grad_out, grad_gate_up, grad_down = (
        lax.psum(grad_qkv.astype(jnp.bfloat16), "dp").astype(jnp.float32),
        lax.psum(grad_out.astype(jnp.bfloat16), "dp").astype(jnp.float32),
        lax.psum(grad_gate_up.astype(jnp.bfloat16), "dp").astype(jnp.float32),
        lax.psum(grad_down.astype(jnp.bfloat16), "dp").astype(jnp.float32),
    )
    root_scale = lax.rsqrt(token_total)
    return (
        output,
        grad_rows,
        grad_qkv * root_scale,
        grad_out * root_scale,
        grad_gate_up * root_scale,
        grad_down * root_scale,
        grad_gain_attn * root_scale,
        grad_gain_mlp * root_scale,
        grad_table * root_scale,
    )


def solution(mesh):
    return jax.shard_map(
        body,
        mesh=mesh,
        in_specs=(
            P(("dp", "mp"), None),
            P("dp"),
            P(("dp", "mp")),
            P(),
            P(),
            P(),
            P(None, None, "mp"),
            P("mp", None),
            P(None, None, "mp"),
            P("mp", None),
            P(("dp", "mp"), None),
        ),
        out_specs=(
            P(("dp", "mp"), None),
            P(("dp", "mp"), None),
            P(None, None, "mp"),
            P("mp", None),
            P(None, None, "mp"),
            P("mp", None),
            P(),
            P(),
            P(),
        ),
        check_vma=False,
    )
```

profile of v0, /device:TPU:0, one launch (start us, length us, event | category | flops | bytes accessed | tf_op | source)
XLA Modules:
  0.0 1067.2 jit_solution(17084121526547978977)
XLA Ops:
  8.1 3.2 multiply_reduce_fusion.2
  11.3 1.7 multiply_convert_fusion.5
  13.6 5.8 fusion.48
  19.4 36.9 %all-gather.5.cloned.1.call-done = bf16[2048,1280]{1,0:T(8,128)(2,1)} async-done(((bf16[512,1280]{1,0:T(8,128)(2,1)}), bf16[2048,1280]{1,0:T(8,128)(2,1)}) %all-gather.5.cloned.1.call-update) | async-done | bytes 5242896 | tf_op jit(solution)/shard_map/all_gather | solution.py:85
  56.3 8.7 fusion.10
  66.2 3.0 fusion.61
  69.2 4.9 reshape.176
  74.1 4.7 copy.39
  78.8 5.3 reshape.177
  84.1 5.5 fusion.62
  89.6 4.9 copy.73
  94.5 4.9 copy.72
  99.3 5.3 reshape.178
  104.7 5.5 fusion.63
  110.1 4.9 copy.75
  115.0 4.9 copy.74
  119.9 7.9 subtract_convert_fusion.3
  127.9 3.2 fusion.64
  132.5 1.8 copy-done.20
  135.5 3.3 copy.41
  138.7 4.3 convert_element_type.131
  143.1 7.1 convolution_convert_fusion.2
  150.3 51.5 %reduce-scatter.5.cloned.1.call-done = bf16[512,1280]{1,0:T(8,128)(2,1)} async-done(((bf16[2048,1280]{1,0:T(8,128)(2,1)}), bf16[512,1280]{1,0:T(8,128)(2,1)}) %reduce-scatter.5.cloned.1.call-update) | async-done | bytes 1310736 | tf_op jit(solution)/shard_map/reduce_scatter | solution.py:102
  201.8 1.8 multiply_reduce_fusion.1
  208.6 38.5 %all-gather.7.cloned.1.call-done = bf16[2048,1280]{1,0:T(8,128)(2,1)} async-done(((bf16[512,1280]{1,0:T(8,128)(2,1)}), bf16[2048,1280]{1,0:T(8,128)(2,1)}) %all-gather.7.cloned.1.call-update) | async-done | bytes 5242896 | tf_op jit(solution)/shard_map/all_gather | solution.py:106
  247.0 22.6 %convolution_bitcast_fusion = f32[2,2048,1280]{2,1,0:T(8,128)} fusion(bf16[2048,1280]{1,0:T(8,128)(2,1)} %all-gather.7.cloned.1.call-done, f32[2,1280,1280]{2,1,0:T(8,128)} %param.19), kind=kOutput, calls=%fused_computation.1 | convolution fusion | flops 13425049600 | bytes 39321600 | tf_op jit(solution)/shard_map/td,cdf->ctf/dot_general | solution.py:108
  269.6 20.0 %all-gather.9.cloned.1.call-done = bf16[2048,1280]{1,0:T(8,128)(2,1)} async-done(((bf16[512,1280]{1,0:T(8,128)(2,1)}), bf16[2048,1280]{1,0:T(8,128)(2,1)}) %all-gather.9.cloned.1.call-update) | async-done | bytes 5242896 | tf_op jit(solution)/shard_map/all_gather | solution.py:120
  289.6 21.7 %fusion.9 = (bf16[1,2048,1280]{2,1,0:T(8,128)(2,1)}, bf16[1,2048,1280]{2,1,0:T(8,128)(2,1)}, bf16[2048,1280]{1,0:T(8,128)(2,1)}) fusion(f32[2,2048,1280]{2,1,0:T(8,128)} %convolution_bitcast_fusion, bf16[2048,1280]{1,0:T(8,128)(2,1)} %all-gather.9.cloned.1.call-done, f32[1280,1280]{1,0:T(8,128)} %param.20), kind=kOutput, calls=%fused_computation.25 | convolution fusion | flops 6751846400 | bytes 48496640 | tf_op jit(solution)/shard_map/td,fd->tf/dot_general | solution.py:122
  311.2 21.7 %bitcast_convert_fusion.1 = bf16[2048,1280]{1,0:T(8,128)(2,1)} fusion(bf16[1,2048,1280]{2,1,0:T(8,128)(2,1)} %get-tuple-element.46, bf16[1,2048,1280]{2,1,0:T(8,128)(2,1)} %get-tuple-element.45, f32[2,1280,1280]{2,1,0:T(8,128)} %param.19), kind=kOutput, calls=%fused_computation.7 | convolution fusion | flops 13432913920 | bytes 28835840 | tf_op jit(solution)/shard_map/ctf,cdf->td/dot_general | solution.py:131
  333.0 12.4 %convolution_convert_fusion.1 = bf16[2048,1280]{1,0:T(8,128)(2,1)} fusion(bf16[2048,1280]{1,0:T(8,128)(2,1)} %get-tuple-element.47, f32[1280,1280]{1,0:T(8,128)} %param.20), kind=kOutput, calls=%fused_computation.14 | convolution fusion | flops 6715146240 | bytes 17039360 | tf_op jit(solution)/shard_map/dot_general | solution.py:115
  345.4 39.1 %reduce-scatter.9.cloned.1.call-done = bf16[512,1280]{1,0:T(8,128)(2,1)} async-done(((bf16[2048,1280]{1,0:T(8,128)(2,1)}), bf16[512,1280]{1,0:T(8,128)(2,1)}) %reduce-scatter.9.cloned.1.call-update) | async-done | bytes 1310736 | tf_op jit(solution)/shard_map/reduce_scatter | solution.py:134
  384.5 2.1 fusion.33
  386.7 51.7 %reduce-scatter.7.cloned.1.call-done = bf16[512,1280]{1,0:T(8,128)(2,1)} async-done(((bf16[2048,1280]{1,0:T(8,128)(2,1)}), bf16[512,1280]{1,0:T(8,128)(2,1)}) %reduce-scatter.7.cloned.1.call-update) | async-done | bytes 1310736 | tf_op jit(solution)/shard_map/reduce_scatter | solution.py:116
  438.4 6.3 fusion.59
  444.8 40.5 %all-gather.11.cloned.1.call-done = bf16[2048,1280]{1,0:T(8,128)(2,1)} async-done(((bf16[512,1280]{1,0:T(8,128)(2,1)}), bf16[2048,1280]{1,0:T(8,128)(2,1)}) %all-gather.11.cloned.1.call-update) | async-done | bytes 5242896 | tf_op jit(solution)/shard_map/all_gather | solution.py:139
  485.3 4.9 convolution_convert_fusion.5
  490.2 4.0 reshape.179
  494.2 3.6 copy.43
  497.8 4.5 convert_bitcast_fusion
  508.1 1.8 multiply_bitcast_fusion.1
  509.9 4.7 subtract_convert_fusion
  514.6 2.5 pad_maximum_fusion.6
  517.1 5.0 copy.59
  522.1 3.1 reshape.174
  525.2 5.0 copy.60
  530.1 2.9 reshape.175
  533.0 4.7 pad_maximum_fusion.5
  537.7 5.0 copy.58
  542.6 2.9 reshape.173
  548.6 1.9 copy-done.28
  550.5 9.9 bitcast_convert_fusion
  560.5 12.3 %convolution_convert_fusion.3 = bf16[1280,1280]{1,0:T(8,128)(2,1)} fusion(bf16[2048,1280]{1,0:T(8,128)(2,1)} %get-tuple-element.47, bf16[2048,1280]{1,0:T(8,128)(2,1)} %all-gather.9.cloned.1.call-done), kind=kOutput, calls=%fused_computation.16 | convolution fusion | flops 6712524800 | bytes 13762560 | tf_op jit(solution)/shard_map/tf,td->fd/dot_general | solution.py:121
  572.8 20.2 %fusion.1 = bf16[2,1280,1280]{1,2,0:T(8,128)(2,1)} fusion(bf16[1,2048,1280]{2,1,0:T(8,128)(2,1)} %get-tuple-element.46, bf16[1,2048,1280]{2,1,0:T(8,128)(2,1)} %get-tuple-element.45, bf16[2048,1280]{1,0:T(8,128)(2,1)} %all-gather.7.cloned.1.call-done), kind=kOutput, calls=%fused_computation.13 | convolution fusion | flops 13430292480 | bytes 22282240 | tf_op jit(solution)/shard_map/td,ctf->cdf/dot_general | solution.py:128
  593.1 2.8 convolution_convert_fusion.4
  595.9 6.5 fusion.20
  602.5 9.5 reduce-scatter.11.cloned.1.call-done
  612.0 2.3 fusion.34
  617.7 44.2 %all-reduce = (f32[]{:T(128)}, f32[1280]{0:T(1024)S(1)}, f32[1280]{0:T(1024)S(1)}, f32[3,1280]{1,0:T(4,128)S(1)}) all-reduce(f32[]{:T(128)} %get-tuple-element.39, f32[1280]{0:T(1024)S(1)} %get-tuple-element.29, f32[1280]{0:T(1024)S(1)} %get-tuple-element.27, f32[3,1280]{1,0:T(4,128)S(1)} %fusion.49), channel_id=1, replica_groups=mesh['dp'=8,'mp'=4] {'dp','mp'}, use_global_device_ids=true, to_apply=%region_13.14 | all-reduce | flops 6401 | bytes 51208 | tf_op jit(solution)/shard_map/psum | solution.py:175
  664.4 365.7 %all-reduce.4.cloned.1.call-done = (bf16[3,1280,320]{1,2,0:T(8,128)(2,1)}, bf16[320,1280]{1,0:T(8,128)(2,1)}, bf16[2,1280,1280]{1,2,0:T(8,128)(2,1)}, bf16[1280,1280]{1,0:T(8,128)(2,1)}) async-done(((bf16[3,1280,320]{1,2,0:T(8,128)(2,1)}, bf16[320,1280]{1,0:T(8,128)(2,1)}, bf16[2,1280,1280]{1,2,0:T(8,128)(2,1)}, bf16[1280,1280]{1,0:T(8,128)(2,1)}), (bf16[3,1280,320]{1,2,0:T(8,128)(2,1)}, ...) | async-done | bytes 13107216 | tf_op jit(solution)/shard_map/psum | solution.py:179
  1030.2 2.6 convert_multiply_fusion.7
  1032.7 2.9 convert_multiply_fusion.2
  1036.0 3.7 convert_multiply_fusion.1
  1040.7 5.8 convert_multiply_fusion
  1046.5 13.9 %copy.54 = f32[2,1280,1280]{2,1,0:T(8,128)} copy(f32[2,1280,1280]{1,2,0:T(8,128)} %convert_multiply_fusion) | data formatting | bytes 26214400
  (138 shorter events, 26.0 us)
Async XLA Ops:
  7.2 0.9 copy-start
  7.2 4.1 copy-start.31
  7.2 49.1 %all-gather.5.cloned.1.call-start = ((), (), s32[]{:S(2)}) async-start(), calls=%async_computation.4 | async-start | bytes 6553600 | tf_op jit(solution)/shard_map/all_gather | solution.py:85
  8.1 4.9 copy-start.35
  11.3 190.5 %copy-start.4 = (f32[512,1280]{1,0:T(8,128)}, f32[512,1280]{1,0:T(8,128)S(1)}, u32[]{:S(2)}) copy-start(f32[512,1280]{1,0:T(8,128)S(1)} %get-tuple-element.73) | copy-start | bytes 7864324
  11.3 1.8 copy-start.37
  11.3 1.8 copy-start.33
  13.0 188.8 %reduce-scatter.5.cloned.1.call-start = ((), (), s32[]{:S(2)}) async-start(), calls=%async_computation.5 | async-start | bytes 6553600 | tf_op jit(solution)/shard_map/reduce_scatter | solution.py:102
  127.9 3.3 copy-start.8
  127.9 3.3 copy-start.10
  127.9 3.3 copy-start.12
  127.9 3.3 copy-start.14
  131.2 4.3 copy-start.2
  131.2 3.1 copy-start.20
  150.2 54.8 %copy-start.30 = (f32[1280]{0:T(1024)S(1)}, f32[1280]{0:T(1024)}, u32[]{:S(2)}) copy-start(f32[1280]{0:T(1024)} %param.16) | copy-start | bytes 15364
  150.2 96.8 %all-gather.7.cloned.1.call-start = ((), (), s32[]{:S(2)}) async-start(), calls=%async_computation.6 | async-start | bytes 6553600 | tf_op jit(solution)/shard_map/all_gather | solution.py:106
  203.6 1.5 copy-start.6
  203.6 3.7 copy-start.18
  206.4 83.1 %all-gather.9.cloned.1.call-start = ((), (), s32[]{:S(2)}) async-start(), calls=%async_computation.8 | async-start | bytes 6553600 | tf_op jit(solution)/shard_map/all_gather | solution.py:120
  208.5 176.0 %reduce-scatter.9.cloned.1.call-start = ((), (), s32[]{:S(2)}) async-start(), calls=%async_computation.9 | async-start | bytes 6553600 | tf_op jit(solution)/shard_map/reduce_scatter | solution.py:134
  333.0 105.4 %reduce-scatter.7.cloned.1.call-start = ((), (), s32[]{:S(2)}) async-start(), calls=%async_computation.7 | async-start | bytes 6553600 | tf_op jit(solution)/shard_map/reduce_scatter | solution.py:116
  345.4 39.1 %copy-start.7 = (f32[512,1280]{1,0:T(8,128)S(1)}, f32[512,1280]{1,0:T(8,128)}, u32[]{:S(2)}) copy-start(f32[512,1280]{1,0:T(8,128)} %copy-done.6) | copy-start | bytes 7864324
  345.4 139.9 %all-gather.11.cloned.1.call-start = ((), (), s32[]{:S(2)}) async-start(), calls=%async_computation.10 | async-start | bytes 6553600 | tf_op jit(solution)/shard_map/all_gather | solution.py:139
  444.7 167.3 %reduce-scatter.11.cloned.1.call-start = ((), (), s32[]{:S(2)}) async-start(), calls=%async_computation.11 | async-start | bytes 6553600 | tf_op jit(solution)/shard_map/reduce_scatter | solution.py:169
  497.8 4.5 copy-start.3
  497.8 4.5 copy-start.21
  503.7 1.6 copy-start.13
  503.7 2.2 copy-start.15
  505.9 1.6 copy-start.9
  505.9 2.2 copy-start.11
  508.1 1.8 copy-start.19
  508.1 1.8 copy-start.24
  545.5 2.9 copy-start.23
  548.5 1.9 copy-start.28
  560.4 469.8 %all-reduce.4.cloned.1.call-start = ((), (), s32[]{:S(2)}) async-start(), calls=%async_computation.12 | async-start | bytes 26214400 | tf_op jit(solution)/shard_map/psum | solution.py:179
  560.4 32.6 %slice-start.4 = ((s8[5242880]{0:T(1024)(128)(4,1)}), s8[4194304]{0:T(1024)(128)(4,1)S(1)}, s32[]{:S(2)}) async-start(s8[5242880]{0:T(1024)(128)(4,1)} %bitcast.110), calls=%async_computation.17 | async-start | bytes 8388608
  560.5 35.5 %slice-start.2 = ((s8[5242880]{0:T(1024)(128)(4,1)}), s8[4194304]{0:T(1024)(128)(4,1)S(1)}, s32[]{:S(2)}) async-start(s8[5242880]{0:T(1024)(128)(4,1)} %bitcast.108), calls=%async_computation.15 | async-start | bytes 8388608
  572.8 20.3 %copy-start.27 = (bf16[2048,320]{1,0:T(8,128)(2,1)S(1)}, bf16[2048,320]{1,0:T(8,128)(2,1)}, u32[]{:S(2)}) copy-start(bf16[2048,320]{1,0:T(8,128)(2,1)} %convert_element_type.131) | copy-start | bytes 3932164
  572.8 20.3 %slice-start.5 = ((s8[5242880]{0:T(1024)(128)(4,1)}), s8[1048576]{0:T(1024)(128)(4,1)S(1)}, s32[]{:S(2)}) async-start(s8[5242880]{0:T(1024)(128)(4,1)} %bitcast.110), calls=%async_computation.18 | async-start | bytes 2097152
  572.8 23.1 %slice-start.3 = ((s8[5242880]{0:T(1024)(128)(4,1)}), s8[1048576]{0:T(1024)(128)(4,1)S(1)}, s32[]{:S(2)}) async-start(s8[5242880]{0:T(1024)(128)(4,1)} %bitcast.108), calls=%async_computation.16 | async-start | bytes 2097152
  593.1 2.8 copy-start.29
  602.5 9.5 copy-start.5
  602.5 9.5 copy-start.32
  602.5 9.5 copy-start.34
  612.0 2.3 copy-start.17
  612.0 2.5 copy-start.22
  614.5 2.2 copy-start.36
  615.1 1.5 copy-start.16
  1030.2 2.6 copy-start.26
  1032.7 3.3 copy-start.25
  1032.7 7.0 slice-start
  1036.0 4.7 slice-start.1
  1046.5 13.9 %copy-start.1 = (f32[3,1280]{1,0:T(4,128)S(1)}, f32[3,1280]{1,0:T(4,128)}, u32[]{:S(2)}) copy-start(f32[3,1280]{1,0:T(4,128)} %param.14) | copy-start | bytes 46084
Sparse Core Ops, SparseCore 0:
  13.1 43.1 all-gather.4
  150.3 51.3 reduce-scatter.4
  206.5 40.4 all-gather.6
  249.1 40.4 all-gather.8
  333.1 51.3 reduce-scatter.8
  386.9 51.3 reduce-scatter.6
  444.8 40.4 all-gather.10
  560.5 51.3 reduce-scatter.10
  617.3 412.7 all-reduce.3
where the time goes:
time: 1080 us; the launch traced here: 1070 us
  waiting for transfers between devices  653 us (60%)
  matrix products  168 us (16%)
  local copies, waits for them, and re-layouts  122 us (11%)
  other arithmetic  63.7 us (6%)
  blocking collectives  44.2 us (4%)
  between operations  15.3 us (1%)
    psum x1, waiting for transfers between devices, body(): lax.psum(grad_qkv.astype(jnp.bfloat16), 'dp').astype(jnp.float32)  366 us
    reduce_scatter x1, waiting for transfers between devices, body(): lax.psum_scatter(mlp_part.astype(jnp.bfloat16), 'mp', scatter_dimension=0...  51.7 us
    reduce_scatter x1, waiting for transfers between devices, body(): lax.psum_scatter(attn_part.astype(jnp.bfloat16), 'mp', scatter_dimension=...  51.5 us
    unnamed x95, local copies, waits for them, and re-layouts  46.5 us
    psum x1, blocking collectives, body(): lax.psum((grad_gain_attn, grad_gain_mlp, grad_table, jnp.sum(mine_valid))...  44.2 us
    all_gather x1, waiting for transfers between devices, body(): lax.all_gather(grad_after.astype(jnp.bfloat16), 'mp', axis=0, tiled=True)  40.5 us
    reduce_scatter x1, waiting for transfers between devices, body(): lax.psum_scatter(mlp_back_part.astype(jnp.bfloat16), 'mp', scatter_dimens...  39.1 us
    all_gather x1, waiting for transfers between devices, body(): normed_mlp = lax.all_gather(normed_mlp_mine, 'mp', axis=0, tiled=True)  38.5 us
  transfers between devices with their start and end apart: 9, of which 9 were waited for; matrix products, arithmetic and copies ran while one was open for 9% of the time, Pallas kernels for 0%

commit v1 on v0

--- a/solution.py
+++ b/solution.py
@@ -82,7 +82,12 @@
     onehot = (classes[:, None] == jnp.arange(NFREQ, dtype=jnp.int32)[None, :]).astype(jnp.float32)
     start_rows = rows + jnp.dot(onehot, freq_table, precision=HIGHEST)
     normed_mine, inverse_attn = norm_forward(start_rows, gain_attn)
-    normed = lax.all_gather(normed_mine, "mp", axis=0, tiled=True)
+    ring = [normed_mine]
+    for hop in range(3):
+        ring.append(lax.ppermute(ring[-1], "mp", [(dev, (dev + 1) % 4) for dev in range(4)]))
+    normed = jnp.roll(
+        jnp.concatenate(ring[::-1], axis=0), (lax.axis_index("mp") + 1) * ring[0].shape[0], axis=0
+    )
     qkv_low = w_qkv.astype(jnp.bfloat16)
     projected = jnp.einsum("td,cdf->ctf", normed, qkv_low, preferred_element_type=jnp.float32)
     projected = projected.reshape(3, series_count, SEQ, head_count, HS)

time: 1080 us -> 1090 us (level)
  waiting for transfers between devices: 653 us -> 664 us
    ppermute x0 -> x3, waiting for transfers between devices: none -> 45.4 us  [body(): lax.ppermute(ring[-1], 'mp', [(dev, (dev + 1) % 4) for dev in range(4)])]
    all_gather x1 -> x0, waiting for transfers between devices: 36.9 us -> none  [body(): normed = lax.all_gather(normed_mine, 'mp', axis=0, tiled=True)]
    unnamed x95 -> x109, local copies, waits for them, and re-layouts: 46.5 us -> 52.8 us
  transfers between devices with their start and end apart: 9 -> 11, of which waited for: 9 -> 11; matrix products, arithmetic and copies ran while one was open for 9% -> 9% of each run, Pallas kernels for 0% -> 0%
where the time goes in v1:
time: 1090 us; the launch traced here: 1080 us
  waiting for transfers between devices  664 us (61%)
  matrix products  165 us (15%)
  local copies, waits for them, and re-layouts  128 us (12%)
  other arithmetic  63.3 us (6%)
  blocking collectives  44.2 us (4%)
  between operations  15.7 us (1%)
    psum x1, waiting for transfers between devices, body(): lax.psum(grad_qkv.astype(jnp.bfloat16), 'dp').astype(jnp.float32)  366 us
    reduce_scatter x1, waiting for transfers between devices, body(): lax.psum_scatter(attn_part.astype(jnp.bfloat16), 'mp', scatter_dimension=...  53.5 us
    unnamed x109, local copies, waits for them, and re-layouts  52.8 us
    reduce_scatter x1, waiting for transfers between devices, body(): lax.psum_scatter(mlp_part.astype(jnp.bfloat16), 'mp', scatter_dimension=0...  51.7 us
    ppermute x3, waiting for transfers between devices, body(): lax.ppermute(ring[-1], 'mp', [(dev, (dev + 1) % 4) for dev in range(4)])  45.4 us
    psum x1, blocking collectives, body(): lax.psum((grad_gain_attn, grad_gain_mlp, grad_table, jnp.sum(mine_valid))...  44.2 us
    all_gather x1, waiting for transfers between devices, body(): lax.all_gather(grad_after.astype(jnp.bfloat16), 'mp', axis=0, tiled=True)  40.5 us
    reduce_scatter x1, waiting for transfers between devices, body(): lax.psum_scatter(mlp_back_part.astype(jnp.bfloat16), 'mp', scatter_dimens...  39.1 us
  transfers between devices with their start and end apart: 11, of which 11 were waited for; matrix products, arithmetic and copies ran while one was open for 9% of the time, Pallas kernels for 0%

profile of v1, /device:TPU:0, one launch (start us, length us, event | category | flops | bytes accessed | tf_op | source)
XLA Modules:
  0.0 1081.1 jit_solution(8714242570282082349)
XLA Ops:
  8.1 3.2 multiply_reduce_fusion.2
  12.1 17.4 %collective-permute-done = bf16[512,1280]{1,0:T(8,128)(2,1)} collective-permute-done((bf16[512,1280]{1,0:T(8,128)(2,1)S(1)}, bf16[512,1280]{1,0:T(8,128)(2,1)}, u32[]{:S(2)}, u32[]{:S(2)}) %collective-permute-start) | collective-permute-done | bytes 1310752 | tf_op jit(solution)/shard_map/ppermute | solution.py:87
  29.5 17.3 %collective-permute-done.1 = bf16[512,1280]{1,0:T(8,128)(2,1)} collective-permute-done((bf16[512,1280]{1,0:T(8,128)(2,1)}, bf16[512,1280]{1,0:T(8,128)(2,1)}, u32[]{:S(2)}, u32[]{:S(2)}) %collective-permute-start.1) | collective-permute-done | bytes 1310752 | tf_op jit(solution)/shard_map/ppermute | solution.py:87
  47.4 6.0 fusion.50
  53.3 10.8 collective-permute-done.2
  70.7 5.3 fusion.12
  77.3 3.0 fusion.65
  80.3 4.9 reshape.176
  85.2 4.7 copy.39
  89.8 5.3 reshape.177
  95.2 5.5 fusion.66
  100.6 4.9 copy.73
  105.5 4.9 copy.72
  110.4 5.3 reshape.178
  115.8 5.5 fusion.67
  121.2 5.0 copy.75
  126.2 4.9 copy.74
  131.1 8.1 subtract_convert_fusion.3
  139.3 3.0 fusion.68
  143.8 1.8 copy-done.20
  146.8 3.3 copy.41
  150.1 4.3 convert_element_type.131
  154.4 7.1 convolution_convert_fusion.2
  161.6 53.5 %reduce-scatter.5.cloned.1.call-done = bf16[512,1280]{1,0:T(8,128)(2,1)} async-done(((bf16[2048,1280]{1,0:T(8,128)(2,1)}), bf16[512,1280]{1,0:T(8,128)(2,1)}) %reduce-scatter.5.cloned.1.call-update) | async-done | bytes 1310736 | tf_op jit(solution)/shard_map/reduce_scatter | solution.py:107
  215.1 1.8 multiply_reduce_fusion.1
  221.9 38.4 %all-gather.4.cloned.1.call-done = bf16[2048,1280]{1,0:T(8,128)(2,1)} async-done(((bf16[512,1280]{1,0:T(8,128)(2,1)}), bf16[2048,1280]{1,0:T(8,128)(2,1)}) %all-gather.4.cloned.1.call-update) | async-done | bytes 5242896 | tf_op jit(solution)/shard_map/all_gather | solution.py:111
  260.3 22.8 %convolution_bitcast_fusion = f32[2,2048,1280]{2,1,0:T(8,128)} fusion(bf16[2048,1280]{1,0:T(8,128)(2,1)} %all-gather.4.cloned.1.call-done, f32[2,1280,1280]{2,1,0:T(8,128)} %param.19), kind=kOutput, calls=%fused_computation.1 | convolution fusion | flops 13425049600 | bytes 39321600 | tf_op jit(solution)/shard_map/td,cdf->ctf/dot_general | solution.py:113
  283.1 19.9 %all-gather.6.cloned.1.call-done = bf16[2048,1280]{1,0:T(8,128)(2,1)} async-done(((bf16[512,1280]{1,0:T(8,128)(2,1)}), bf16[2048,1280]{1,0:T(8,128)(2,1)}) %all-gather.6.cloned.1.call-update) | async-done | bytes 5242896 | tf_op jit(solution)/shard_map/all_gather | solution.py:125
  303.0 21.7 %fusion.9 = (bf16[1,2048,1280]{2,1,0:T(8,128)(2,1)}, bf16[1,2048,1280]{2,1,0:T(8,128)(2,1)}, bf16[2048,1280]{1,0:T(8,128)(2,1)}) fusion(f32[2,2048,1280]{2,1,0:T(8,128)} %convolution_bitcast_fusion, bf16[2048,1280]{1,0:T(8,128)(2,1)} %all-gather.6.cloned.1.call-done, f32[1280,1280]{1,0:T(8,128)} %param.20), kind=kOutput, calls=%fused_computation.25 | convolution fusion | flops 6751846400 | bytes 48496640 | tf_op jit(solution)/shard_map/td,fd->tf/dot_general | solution.py:127
  324.7 21.5 %bitcast_convert_fusion.1 = bf16[2048,1280]{1,0:T(8,128)(2,1)} fusion(bf16[1,2048,1280]{2,1,0:T(8,128)(2,1)} %get-tuple-element.46, bf16[1,2048,1280]{2,1,0:T(8,128)(2,1)} %get-tuple-element.45, f32[2,1280,1280]{2,1,0:T(8,128)} %param.19), kind=kOutput, calls=%fused_computation.7 | convolution fusion | flops 13432913920 | bytes 28835840 | tf_op jit(solution)/shard_map/ctf,cdf->td/dot_general | solution.py:136
  346.3 12.4 %convolution_convert_fusion.1 = bf16[2048,1280]{1,0:T(8,128)(2,1)} fusion(bf16[2048,1280]{1,0:T(8,128)(2,1)} %get-tuple-element.47, f32[1280,1280]{1,0:T(8,128)} %param.20), kind=kOutput, calls=%fused_computation.14 | convolution fusion | flops 6715146240 | bytes 17039360 | tf_op jit(solution)/shard_map/dot_general | solution.py:120
  358.7 39.1 %reduce-scatter.9.cloned.1.call-done = bf16[512,1280]{1,0:T(8,128)(2,1)} async-done(((bf16[2048,1280]{1,0:T(8,128)(2,1)}), bf16[512,1280]{1,0:T(8,128)(2,1)}) %reduce-scatter.9.cloned.1.call-update) | async-done | bytes 1310736 | tf_op jit(solution)/shard_map/reduce_scatter | solution.py:139
  397.8 2.1 fusion.35
  399.9 51.7 %reduce-scatter.7.cloned.1.call-done = bf16[512,1280]{1,0:T(8,128)(2,1)} async-done(((bf16[2048,1280]{1,0:T(8,128)(2,1)}), bf16[512,1280]{1,0:T(8,128)(2,1)}) %reduce-scatter.7.cloned.1.call-update) | async-done | bytes 1310736 | tf_op jit(solution)/shard_map/reduce_scatter | solution.py:121
  451.6 6.3 fusion.63
  458.0 40.5 %all-gather.8.cloned.1.call-done = bf16[2048,1280]{1,0:T(8,128)(2,1)} async-done(((bf16[512,1280]{1,0:T(8,128)(2,1)}), bf16[2048,1280]{1,0:T(8,128)(2,1)}) %all-gather.8.cloned.1.call-update) | async-done | bytes 5242896 | tf_op jit(solution)/shard_map/all_gather | solution.py:144
  498.5 4.9 convolution_convert_fusion.5
  503.4 4.1 reshape.179
  507.5 3.6 copy.43
  511.1 4.5 convert_bitcast_fusion
  523.2 4.7 subtract_convert_fusion
  527.9 2.5 pad_maximum_fusion.6
  530.4 5.0 copy.59
  535.4 3.3 reshape.174
  538.7 5.0 copy.60
  543.6 2.9 reshape.175
  546.5 4.7 pad_maximum_fusion.5
  551.3 5.0 copy.58
  556.2 2.9 reshape.173
  562.1 1.9 copy-done.28
  564.0 9.9 bitcast_convert_fusion
  574.0 12.0 %convolution_convert_fusion.3 = bf16[1280,1280]{1,0:T(8,128)(2,1)} fusion(bf16[2048,1280]{1,0:T(8,128)(2,1)} %get-tuple-element.47, bf16[2048,1280]{1,0:T(8,128)(2,1)} %all-gather.6.cloned.1.call-done), kind=kOutput, calls=%fused_computation.16 | convolution fusion | flops 6712524800 | bytes 13762560 | tf_op jit(solution)/shard_map/tf,td->fd/dot_general | solution.py:126
  586.1 20.3 %fusion.1 = bf16[2,1280,1280]{1,2,0:T(8,128)(2,1)} fusion(bf16[1,2048,1280]{2,1,0:T(8,128)(2,1)} %get-tuple-element.46, bf16[1,2048,1280]{2,1,0:T(8,128)(2,1)} %get-tuple-element.45, bf16[2048,1280]{1,0:T(8,128)(2,1)} %all-gather.4.cloned.1.call-done), kind=kOutput, calls=%fused_computation.13 | convolution fusion | flops 13430292480 | bytes 22282240 | tf_op jit(solution)/shard_map/td,ctf->cdf/dot_general | solution.py:133
  606.5 2.8 convolution_convert_fusion.4
  609.3 6.5 fusion.22
  615.9 9.7 reduce-scatter.11.cloned.1.call-done
  625.6 2.3 fusion.36
  631.3 44.2 %all-reduce = (f32[]{:T(128)}, f32[1280]{0:T(1024)S(1)}, f32[1280]{0:T(1024)S(1)}, f32[3,1280]{1,0:T(4,128)S(1)}) all-reduce(f32[]{:T(128)} %get-tuple-element.39, f32[1280]{0:T(1024)S(1)} %get-tuple-element.29, f32[1280]{0:T(1024)S(1)} %get-tuple-element.27, f32[3,1280]{1,0:T(4,128)S(1)} %fusion.51), channel_id=1, replica_groups=mesh['dp'=8,'mp'=4] {'dp','mp'}, use_global_device_ids=true, to_apply=%region_13.14 | all-reduce | flops 6401 | bytes 51208 | tf_op jit(solution)/shard_map/psum | solution.py:180
  678.0 365.7 %all-reduce.4.cloned.1.call-done = (bf16[3,1280,320]{1,2,0:T(8,128)(2,1)}, bf16[320,1280]{1,0:T(8,128)(2,1)}, bf16[2,1280,1280]{1,2,0:T(8,128)(2,1)}, bf16[1280,1280]{1,0:T(8,128)(2,1)}) async-done(((bf16[3,1280,320]{1,2,0:T(8,128)(2,1)}, bf16[320,1280]{1,0:T(8,128)(2,1)}, bf16[2,1280,1280]{1,2,0:T(8,128)(2,1)}, bf16[1280,1280]{1,0:T(8,128)(2,1)}), (bf16[3,1280,320]{1,2,0:T(8,128)(2,1)}, ...) | async-done | bytes 13107216 | tf_op jit(solution)/shard_map/psum | solution.py:184
  1043.7 2.6 convert_multiply_fusion.7
  1046.3 2.9 convert_multiply_fusion.2
  1049.6 3.7 convert_multiply_fusion.1
  1054.3 5.8 convert_multiply_fusion
  1060.1 13.9 %copy.54 = f32[2,1280,1280]{2,1,0:T(8,128)} copy(f32[2,1280,1280]{1,2,0:T(8,128)} %convert_multiply_fusion) | data formatting | bytes 26214400
  (158 shorter events, 35.2 us)
Async XLA Ops:
  7.2 0.9 copy-start
  7.2 4.1 copy-start.30
  7.2 207.9 %reduce-scatter.5.cloned.1.call-start = ((), (), s32[]{:S(2)}) async-start(), calls=%async_computation.4 | async-start | bytes 6553600 | tf_op jit(solution)/shard_map/reduce_scatter | solution.py:107
  8.1 3.6 copy-start.36
  8.1 38.8 %copy-start.38 = (s32[32]{0:T(128)S(1)}, s32[32]{0:T(128)}, u32[]{:S(2)}) copy-start(s32[32]{0:T(128)} %param.12) | copy-start | bytes 388
  11.3 203.9 %copy-start.2 = (f32[512,1280]{1,0:T(8,128)}, f32[512,1280]{1,0:T(8,128)S(1)}, u32[]{:S(2)}) copy-start(f32[512,1280]{1,0:T(8,128)S(1)} %get-tuple-element.73) | copy-start | bytes 7864324
  11.3 59.1 %copy-start.33 = (f32[512]{0:T(512)}, f32[512]{0:T(512)S(1)}, u32[]{:S(2)}) copy-start(f32[512]{0:T(512)S(1)} %add_rsqrt_fusion.1) | copy-start | bytes 6148
  11.6 17.9 %collective-permute-start = (bf16[512,1280]{1,0:T(8,128)(2,1)S(1)}, bf16[512,1280]{1,0:T(8,128)(2,1)}, u32[]{:S(2)}, u32[]{:S(2)}) collective-permute-start(bf16[512,1280]{1,0:T(8,128)(2,1)S(1)} %multiply_convert_fusion.5), channel_id=1, source_target_pairs={{0,1},{1,2},{2,3},{3,0},{4,5},{5,6},{6,7},{7,4},{8,9},{9,10},{10,1... | collective-permute-start | bytes 3932168 | tf_op jit(solution)/shard_map/ppermute | solution.py:87
  29.5 17.3 %collective-permute-start.1 = (bf16[512,1280]{1,0:T(8,128)(2,1)}, bf16[512,1280]{1,0:T(8,128)(2,1)}, u32[]{:S(2)}, u32[]{:S(2)}) collective-permute-start(bf16[512,1280]{1,0:T(8,128)(2,1)} %collective-permute-done), channel_id=1, source_target_pairs={{0,1},{1,2},{2,3},{3,0},{4,5},{5,6},{6,7},{7,4},{8,9},{9,10},{10,1... | collective-permute-start | bytes 3932168 | tf_op jit(solution)/shard_map/ppermute | solution.py:87
  46.8 17.2 %collective-permute-start.2 = (bf16[512,1280]{1,0:T(8,128)(2,1)}, bf16[512,1280]{1,0:T(8,128)(2,1)S(1)}, u32[]{:S(2)}, u32[]{:S(2)}) collective-permute-start(bf16[512,1280]{1,0:T(8,128)(2,1)} %collective-permute-done.1), channel_id=1, source_target_pairs={{0,1},{1,2},{2,3},{3,0},{4,5},{5,6},{6,7},{7,4},{8,9},{9,10},{10,1... | collective-permute-start | bytes 3932168 | tf_op jit(solution)/shard_map/ppermute | solution.py:87
  67.0 3.7 slice-start.7
  67.4 3.3 slice-start.8
  70.7 5.3 copy-start.32
  139.2 3.1 copy-start.8
  139.2 3.1 copy-start.10
  139.2 3.1 copy-start.12
  139.2 3.3 copy-start.14
  142.5 4.3 copy-start.4
  142.5 3.1 copy-start.20
  161.6 56.8 %copy-start.35 = (f32[1280]{0:T(1024)S(1)}, f32[1280]{0:T(1024)}, u32[]{:S(2)}) copy-start(f32[1280]{0:T(1024)} %param.16) | copy-start | bytes 15364
  161.6 98.8 %all-gather.4.cloned.1.call-start = ((), (), s32[]{:S(2)}) async-start(), calls=%async_computation.5 | async-start | bytes 6553600 | tf_op jit(solution)/shard_map/all_gather | solution.py:111
  216.9 1.5 copy-start.6
  216.9 3.6 copy-start.18
  219.8 83.3 %all-gather.6.cloned.1.call-start = ((), (), s32[]{:S(2)}) async-start(), calls=%async_computation.7 | async-start | bytes 6553600 | tf_op jit(solution)/shard_map/all_gather | solution.py:125
  221.8 175.9 %reduce-scatter.9.cloned.1.call-start = ((), (), s32[]{:S(2)}) async-start(), calls=%async_computation.8 | async-start | bytes 6553600 | tf_op jit(solution)/shard_map/reduce_scatter | solution.py:139
  346.2 105.4 %reduce-scatter.7.cloned.1.call-start = ((), (), s32[]{:S(2)}) async-start(), calls=%async_computation.6 | async-start | bytes 6553600 | tf_op jit(solution)/shard_map/reduce_scatter | solution.py:121
  358.6 39.1 %copy-start.7 = (f32[512,1280]{1,0:T(8,128)S(1)}, f32[512,1280]{1,0:T(8,128)}, u32[]{:S(2)}) copy-start(f32[512,1280]{1,0:T(8,128)} %copy-done.6) | copy-start | bytes 7864324
  358.7 139.9 %all-gather.8.cloned.1.call-start = ((), (), s32[]{:S(2)}) async-start(), calls=%async_computation.9 | async-start | bytes 6553600 | tf_op jit(solution)/shard_map/all_gather | solution.py:144
  457.9 167.6 %reduce-scatter.11.cloned.1.call-start = ((), (), s32[]{:S(2)}) async-start(), calls=%async_computation.10 | async-start | bytes 6553600 | tf_op jit(solution)/shard_map/reduce_scatter | solution.py:174
  511.1 4.5 copy-start.5
  511.1 4.5 copy-start.21
  517.0 1.6 copy-start.13
  517.0 2.2 copy-start.15
  519.2 1.6 copy-start.9
  519.2 2.2 copy-start.11
  521.5 1.8 copy-start.19
  521.5 1.8 copy-start.24
  559.1 2.9 copy-start.23
  562.1 1.9 copy-start.28
  574.0 469.7 %all-reduce.4.cloned.1.call-start = ((), (), s32[]{:S(2)}) async-start(), calls=%async_computation.11 | async-start | bytes 26214400 | tf_op jit(solution)/shard_map/psum | solution.py:184
  574.0 32.4 %slice-start.5 = ((s8[5242880]{0:T(1024)(128)(4,1)}), s8[4194304]{0:T(1024)(128)(4,1)S(1)}, s32[]{:S(2)}) async-start(s8[5242880]{0:T(1024)(128)(4,1)} %bitcast.110), calls=%async_computation.17 | async-start | bytes 8388608
  574.0 35.2 %slice-start.2 = ((s8[10485760]{0:T(1024)(128)(4,1)}), s8[4194304]{0:T(1024)(128)(4,1)S(1)}, s32[]{:S(2)}) async-start(s8[10485760]{0:T(1024)(128)(4,1)} %bitcast.108), calls=%async_computation.14 | async-start | bytes 8388608
  586.1 20.4 %copy-start.27 = (bf16[2048,320]{1,0:T(8,128)(2,1)S(1)}, bf16[2048,320]{1,0:T(8,128)(2,1)}, u32[]{:S(2)}) copy-start(bf16[2048,320]{1,0:T(8,128)(2,1)} %convert_element_type.131) | copy-start | bytes 3932164
  586.1 20.4 %slice-start.6 = ((s8[5242880]{0:T(1024)(128)(4,1)}), s8[1048576]{0:T(1024)(128)(4,1)S(1)}, s32[]{:S(2)}) async-start(s8[5242880]{0:T(1024)(128)(4,1)} %bitcast.110), calls=%async_computation.18 | async-start | bytes 2097152
  586.1 23.2 %slice-start.3 = ((s8[10485760]{0:T(1024)(128)(4,1)}), s8[4194304]{0:T(1024)(128)(4,1)S(1)}, s32[]{:S(2)}) async-start(s8[10485760]{0:T(1024)(128)(4,1)} %bitcast.108), calls=%async_computation.15 | async-start | bytes 8388608
  586.1 23.2 %slice-start.4 = ((s8[10485760]{0:T(1024)(128)(4,1)}), s8[2097152]{0:T(1024)(128)(4,1)S(1)}, s32[]{:S(2)}) async-start(s8[10485760]{0:T(1024)(128)(4,1)} %bitcast.108), calls=%async_computation.16 | async-start | bytes 4194304
  606.5 2.8 copy-start.29
  615.8 9.7 copy-start.3
  615.8 9.7 copy-start.31
  615.8 9.7 copy-start.34
  625.5 2.3 copy-start.17
  625.5 2.5 copy-start.22
  628.0 2.2 copy-start.37
  628.7 1.5 copy-start.16
  1043.7 2.6 copy-start.26
  1046.3 3.3 copy-start.25
  1046.3 7.0 slice-start
  1049.6 4.7 slice-start.1
  1060.1 13.9 %copy-start.1 = (f32[3,1280]{1,0:T(4,128)S(1)}, f32[3,1280]{1,0:T(4,128)}, u32[]{:S(2)}) copy-start(f32[3,1280]{1,0:T(4,128)} %param.14) | copy-start | bytes 46084
Sparse Core Ops, SparseCore 0:
  161.7 53.4 reduce-scatter.4
  219.9 40.4 all-gather.3
  262.6 40.4 all-gather.5
  346.3 51.3 reduce-scatter.8
  400.2 51.3 reduce-scatter.6
  458.0 40.4 all-gather.7
  574.1 51.3 reduce-scatter.10
  630.9 412.7 all-reduce.3
